TPU v7x, 256 devices: a whole 4x4x8 slice. The times are simulated.
256 devices in a mesh: cells: 16 (over z, core), lev: 16 (over x, y).
Axes of the slice: x: 4, y: 4, z: 8, core: 2. Of those that a mesh axis runs over, the one named last changes fastest.
Arguments:
- source_levels: float32 [128, 65536], P('lev', 'cells'), may hold values from -6 to 6
- level_to_mode: float32 [128, 128], replicated, may hold values from -0.5 to 0.5
- mode_to_level: float32 [128, 128], replicated, may hold values from -0.5 to 0.5
- mode_shift: float32 [128], P('lev'), may hold values from 0.02 to 1
- edge_weight: float32 [6, 65536], P(None, 'cells'), may hold values from 0.05 to 0.5
- neighbours: int32 [6, 65536], P(None, 'cells'), may hold values from 0 to 6143, as said below
- send_lists: int32 [16, 2048], P('cells'), may hold values from 0 to 4095, as said below
Outputs:
- correction: float32 [128, 65536], P('lev', 'cells')
Inputs may be any that keep to these rules, and one draw needn't show every extreme that they name: `neighbours`: an entry below 4096 is a cell of the same partition whose local index differs from the cell's own local index by at most 32; an entry e of partition p at or above 4096 names halo slot h = (e - 4096) % 128 from partition s = (e - 4096) // 128, with s not p and h below the number of cells that s sends to p. An unused entry names the cell itself. `send_lists`: the number of used slots from partition s to partition q differs from pair to pair: 1 to 128 for every pair of different partitions, 0 for a partition and itself; in every draw some partition receives 128 cells from every other one. Unused slots hold any cell.
All inputs are finite; a program needn't handle non-finite values.
Results may differ from a plain program's by a relative error of at most 0.00007.
Values sent between devices are 32-bit elements; how exact they have to be, the bound alone decides.
A program may use at most 64 MiB of HBM per device.

v0:
```python
import jax
import jax.numpy as jnp
from jax import lax
from jax.sharding import PartitionSpec as P

DEG = 6
HMAX = 128
SWEEPS = 2
STEPS = 4


def full_product(left, right):
    return jnp.dot(left, right, precision=lax.Precision.HIGHEST, preferred_element_type=jnp.float32)


def local(
    source_levels, level_to_mode, mode_to_level, mode_shift, edge_weight, neighbours, send_lists
):
    slab_rows = source_levels.shape[0]
    position = lax.axis_index("lev")
    send_cells = send_lists.reshape(-1)
    slot_total = send_cells.shape[0]
    diagonal = jnp.sum(edge_weight, axis=0)
    own_rows = lax.dynamic_slice_in_dim(level_to_mode, position * slab_rows, slab_rows, 0)
    mode_field = full_product(own_rows, lax.all_gather(source_levels, "lev", axis=0, tiled=True))
    shift_col = mode_shift[:, None]
    own_scale = shift_col + diagonal[None, :]

    def apply_operator(field):
        outgoing = jnp.take(field, send_cells, axis=1)
        arrived = lax.all_to_all(
            outgoing.reshape(slab_rows, -1, HMAX), "cells", split_axis=1, concat_axis=1, tiled=True
        ).reshape(slab_rows, slot_total)
        extended = jnp.concatenate([field, arrived], axis=1)
        running = own_scale * field
        for slot_number in range(DEG):
            running = running - edge_weight[slot_number][None, :] * jnp.take(
                extended, neighbours[slot_number], axis=1
            )
        return running

    radius = DEG / 2.0
    centre = shift_col + radius
    sigma_ratio = centre / radius
    answer = jnp.zeros_like(mode_field)
    remain = mode_field
    direction = jnp.zeros_like(mode_field)
    factor = 1.0 / sigma_ratio
    for sweep_index in range(SWEEPS):
        for step_index in range(STEPS):
            if step_index == 0:
                if sweep_index > 0:
                    remain = remain - apply_operator(direction)
                factor = 1.0 / sigma_ratio
                direction = remain / centre
            else:
                remain = remain - apply_operator(direction)
                newer = 1.0 / (2.0 * sigma_ratio - factor)
                direction = newer * factor * direction + 2.0 * newer / radius * remain
                factor = newer
            answer = answer + direction
    own_columns = lax.dynamic_slice_in_dim(mode_to_level, position * slab_rows, slab_rows, 1)
    return lax.psum_scatter(
        full_product(own_columns, answer), "lev", scatter_dimension=0, tiled=True
    )


def solution(mesh):
    in_specs = (
        P("lev", "cells"),
        P(),
        P(),
        P("lev"),
        P(None, "cells"),
        P(None, "cells"),
        P("cells", None),
    )
    out_specs = P("lev", "cells")
    return jax.shard_map(local, mesh=mesh, in_specs=in_specs, out_specs=out_specs, check_vma=False)
```

profile of v0, /device:TPU:1, one launch (start us, length us, event | category | flops | bytes accessed | tf_op | source)
XLA Modules:
  0.0 1055.3 jit_solution(7952593365196662498)
XLA Ops:
  21.0 41.8 %all-gather.2.cloned.1.call-done = f32[128,4096]{1,0:T(8,128)} async-done(((f32[8,4096]{1,0:T(8,128)}), f32[128,4096]{1,0:T(8,128)}) %all-gather.2.cloned.1.call-update) | async-done | bytes 2097168 | tf_op jit(solution)/shard_map/all_gather | solution.py:25
  93.4 15.4 %gather_fusion.6 = f32[4096,8]{1,0:T(8,128)} fusion(f32[8,6144]{0,1:T(8,128)S(1)} %copy.108, s32[4096]{0:T(1024)} %fusion.90), kind=kCustom, calls=%fused_computation.12.clone | custom fusion | bytes 278528 | tf_op jit(solution)/shard_map/jit(_take)/gather | solution.py:37
  111.6 14.1 %gather_fusion.5 = f32[4096,8]{1,0:T(8,128)} fusion(f32[8,6144]{0,1:T(8,128)S(1)} %copy.108, s32[4096]{0:T(1024)S(1)} %copy-done.49), kind=kCustom, calls=%fused_computation.11.clone | custom fusion | bytes 278528 | tf_op jit(solution)/shard_map/jit(_take)/gather | solution.py:37
  128.5 14.1 %gather_fusion.4 = f32[4096,8]{1,0:T(8,128)} fusion(f32[8,6144]{0,1:T(8,128)S(1)} %copy.108, s32[4096]{0:T(1024)S(1)} %copy-done.47), kind=kCustom, calls=%fused_computation.10.clone | custom fusion | bytes 278528 | tf_op jit(solution)/shard_map/jit(_take)/gather | solution.py:37
  145.4 14.1 %gather_fusion.3 = f32[4096,8]{1,0:T(8,128)} fusion(f32[8,6144]{0,1:T(8,128)S(1)} %copy.108, s32[4096]{0:T(1024)S(1)} %copy-done.45), kind=kCustom, calls=%fused_computation.9.clone | custom fusion | bytes 278528 | tf_op jit(solution)/shard_map/jit(_take)/gather | solution.py:37
  162.4 14.1 %gather_fusion.2 = f32[4096,8]{1,0:T(8,128)} fusion(f32[8,6144]{0,1:T(8,128)S(1)} %copy.108, s32[4096]{0:T(1024)S(1)} %copy-done.41), kind=kCustom, calls=%fused_computation.8.clone | custom fusion | bytes 278528 | tf_op jit(solution)/shard_map/jit(_take)/gather | solution.py:37
  179.3 14.1 %gather_fusion.1 = f32[4096,8]{1,0:T(8,128)} fusion(f32[8,6144]{0,1:T(8,128)S(1)} %copy.108, s32[4096]{0:T(1024)S(1)} %copy-done.43), kind=kCustom, calls=%fused_computation.1.clone | custom fusion | bytes 278528 | tf_op jit(solution)/shard_map/jit(_take)/gather | solution.py:37
  205.3 10.5 all_to_all.35
  218.4 14.1 %gather_fusion.13 = f32[4096,8]{1,0:T(8,128)} fusion(f32[8,6144]{0,1:T(8,128)S(1)} %copy.122, s32[4096]{0:T(1024)S(1)} %copy-done.51), kind=kCustom, calls=%fused_computation.18.clone | custom fusion | bytes 278528 | tf_op jit(solution)/shard_map/jit(_take)/gather | solution.py:37
  232.5 14.1 %gather_fusion.12 = f32[4096,8]{1,0:T(8,128)} fusion(f32[8,6144]{0,1:T(8,128)S(1)} %copy.122, s32[4096]{0:T(1024)S(1)} %copy-done.50), kind=kCustom, calls=%fused_computation.17.clone | custom fusion | bytes 278528 | tf_op jit(solution)/shard_map/jit(_take)/gather | solution.py:37
  246.6 14.1 %gather_fusion.11 = f32[4096,8]{1,0:T(8,128)} fusion(f32[8,6144]{0,1:T(8,128)S(1)} %copy.122, s32[4096]{0:T(1024)S(1)} %copy-done.48), kind=kCustom, calls=%fused_computation.16.clone | custom fusion | bytes 278528 | tf_op jit(solution)/shard_map/jit(_take)/gather | solution.py:37
  260.7 14.1 %gather_fusion.10 = f32[4096,8]{1,0:T(8,128)} fusion(f32[8,6144]{0,1:T(8,128)S(1)} %copy.122, s32[4096]{0:T(1024)S(1)} %copy-done.46), kind=kCustom, calls=%fused_computation.15.clone | custom fusion | bytes 278528 | tf_op jit(solution)/shard_map/jit(_take)/gather | solution.py:37
  274.8 14.1 %gather_fusion.9 = f32[4096,8]{1,0:T(8,128)} fusion(f32[8,6144]{0,1:T(8,128)S(1)} %copy.122, s32[4096]{0:T(1024)S(1)} %copy-done.42), kind=kCustom, calls=%fused_computation.14.clone | custom fusion | bytes 278528 | tf_op jit(solution)/shard_map/jit(_take)/gather | solution.py:37
  288.9 14.1 %gather_fusion.8 = f32[4096,8]{1,0:T(8,128)} fusion(f32[8,6144]{0,1:T(8,128)S(1)} %copy.122, s32[4096]{0:T(1024)S(1)} %copy-done.44), kind=kCustom, calls=%fused_computation.13.clone | custom fusion | bytes 278528 | tf_op jit(solution)/shard_map/jit(_take)/gather | solution.py:37
  337.2 15.4 %gather_fusion.20 = f32[4096,8]{1,0:T(8,128)} fusion(f32[8,6144]{0,1:T(8,128)S(1)} %copy.136, s32[4096]{0:T(1024)} %fusion.90), kind=kCustom, calls=%fused_computation.24.clone | custom fusion | bytes 278528 | tf_op jit(solution)/shard_map/jit(_take)/gather | solution.py:37
  352.6 15.4 %gather_fusion.19 = f32[4096,8]{1,0:T(8,128)} fusion(f32[8,6144]{0,1:T(8,128)S(1)} %copy.136, s32[4096]{0:T(1024)} %fusion.89), kind=kCustom, calls=%fused_computation.23.clone | custom fusion | bytes 278528 | tf_op jit(solution)/shard_map/jit(_take)/gather | solution.py:37
  368.0 15.4 %gather_fusion.18 = f32[4096,8]{1,0:T(8,128)} fusion(f32[8,6144]{0,1:T(8,128)S(1)} %copy.136, s32[4096]{0:T(1024)} %fusion.88), kind=kCustom, calls=%fused_computation.22.clone | custom fusion | bytes 278528 | tf_op jit(solution)/shard_map/jit(_take)/gather | solution.py:37
  383.5 15.4 %gather_fusion.17 = f32[4096,8]{1,0:T(8,128)} fusion(f32[8,6144]{0,1:T(8,128)S(1)} %copy.136, s32[4096]{0:T(1024)} %fusion.87), kind=kCustom, calls=%fused_computation.21.clone | custom fusion | bytes 278528 | tf_op jit(solution)/shard_map/jit(_take)/gather | solution.py:37
  398.9 15.4 %gather_fusion.16 = f32[4096,8]{1,0:T(8,128)} fusion(f32[8,6144]{0,1:T(8,128)S(1)} %copy.136, s32[4096]{0:T(1024)} %fusion.86), kind=kCustom, calls=%fused_computation.20.clone | custom fusion | bytes 278528 | tf_op jit(solution)/shard_map/jit(_take)/gather | solution.py:37
  414.3 15.4 %gather_fusion.15 = f32[4096,8]{1,0:T(8,128)} fusion(f32[8,6144]{0,1:T(8,128)S(1)} %copy.136, s32[4096]{0:T(1024)} %fusion.85), kind=kCustom, calls=%fused_computation.19.clone | custom fusion | bytes 278528 | tf_op jit(solution)/shard_map/jit(_take)/gather | solution.py:37
  452.6 10.4 all_to_all.36
  465.5 15.4 %gather_fusion.27 = f32[4096,8]{1,0:T(8,128)} fusion(f32[8,6144]{0,1:T(8,128)S(1)} %copy.150, s32[4096]{0:T(1024)} %fusion.90), kind=kCustom, calls=%fused_computation.30.clone | custom fusion | bytes 278528 | tf_op jit(solution)/shard_map/jit(_take)/gather | solution.py:37
  480.9 15.4 %gather_fusion.26 = f32[4096,8]{1,0:T(8,128)} fusion(f32[8,6144]{0,1:T(8,128)S(1)} %copy.150, s32[4096]{0:T(1024)} %fusion.89), kind=kCustom, calls=%fused_computation.29.clone | custom fusion | bytes 278528 | tf_op jit(solution)/shard_map/jit(_take)/gather | solution.py:37
  496.3 15.4 %gather_fusion.25 = f32[4096,8]{1,0:T(8,128)} fusion(f32[8,6144]{0,1:T(8,128)S(1)} %copy.150, s32[4096]{0:T(1024)} %fusion.88), kind=kCustom, calls=%fused_computation.28.clone | custom fusion | bytes 278528 | tf_op jit(solution)/shard_map/jit(_take)/gather | solution.py:37
  511.7 15.4 %gather_fusion.24 = f32[4096,8]{1,0:T(8,128)} fusion(f32[8,6144]{0,1:T(8,128)S(1)} %copy.150, s32[4096]{0:T(1024)} %fusion.87), kind=kCustom, calls=%fused_computation.27.clone | custom fusion | bytes 278528 | tf_op jit(solution)/shard_map/jit(_take)/gather | solution.py:37
  527.1 15.4 %gather_fusion.23 = f32[4096,8]{1,0:T(8,128)} fusion(f32[8,6144]{0,1:T(8,128)S(1)} %copy.150, s32[4096]{0:T(1024)} %fusion.86), kind=kCustom, calls=%fused_computation.26.clone | custom fusion | bytes 278528 | tf_op jit(solution)/shard_map/jit(_take)/gather | solution.py:37
  542.6 15.4 %gather_fusion.22 = f32[4096,8]{1,0:T(8,128)} fusion(f32[8,6144]{0,1:T(8,128)S(1)} %copy.150, s32[4096]{0:T(1024)} %fusion.85), kind=kCustom, calls=%fused_computation.25.clone | custom fusion | bytes 278528 | tf_op jit(solution)/shard_map/jit(_take)/gather | solution.py:37
  579.8 10.4 all_to_all.37
  592.7 15.4 %gather_fusion.34 = f32[4096,8]{1,0:T(8,128)} fusion(f32[8,6144]{0,1:T(8,128)S(1)} %copy.164, s32[4096]{0:T(1024)} %fusion.90), kind=kCustom, calls=%fused_computation.36.clone | custom fusion | bytes 278528 | tf_op jit(solution)/shard_map/jit(_take)/gather | solution.py:37
  608.2 15.4 %gather_fusion.33 = f32[4096,8]{1,0:T(8,128)} fusion(f32[8,6144]{0,1:T(8,128)S(1)} %copy.164, s32[4096]{0:T(1024)} %fusion.89), kind=kCustom, calls=%fused_computation.35.clone | custom fusion | bytes 278528 | tf_op jit(solution)/shard_map/jit(_take)/gather | solution.py:37
  623.6 15.4 %gather_fusion.32 = f32[4096,8]{1,0:T(8,128)} fusion(f32[8,6144]{0,1:T(8,128)S(1)} %copy.164, s32[4096]{0:T(1024)} %fusion.88), kind=kCustom, calls=%fused_computation.34.clone | custom fusion | bytes 278528 | tf_op jit(solution)/shard_map/jit(_take)/gather | solution.py:37
  639.0 15.4 %gather_fusion.31 = f32[4096,8]{1,0:T(8,128)} fusion(f32[8,6144]{0,1:T(8,128)S(1)} %copy.164, s32[4096]{0:T(1024)} %fusion.87), kind=kCustom, calls=%fused_computation.33.clone | custom fusion | bytes 278528 | tf_op jit(solution)/shard_map/jit(_take)/gather | solution.py:37
  654.4 15.4 %gather_fusion.30 = f32[4096,8]{1,0:T(8,128)} fusion(f32[8,6144]{0,1:T(8,128)S(1)} %copy.164, s32[4096]{0:T(1024)} %fusion.86), kind=kCustom, calls=%fused_computation.32.clone | custom fusion | bytes 278528 | tf_op jit(solution)/shard_map/jit(_take)/gather | solution.py:37
  669.8 15.4 %gather_fusion.29 = f32[4096,8]{1,0:T(8,128)} fusion(f32[8,6144]{0,1:T(8,128)S(1)} %copy.164, s32[4096]{0:T(1024)} %fusion.85), kind=kCustom, calls=%fused_computation.31.clone | custom fusion | bytes 278528 | tf_op jit(solution)/shard_map/jit(_take)/gather | solution.py:37
  719.4 15.4 %gather_fusion.41 = f32[4096,8]{1,0:T(8,128)} fusion(f32[8,6144]{0,1:T(8,128)S(1)} %copy.178, s32[4096]{0:T(1024)} %fusion.90), kind=kCustom, calls=%fused_computation.42.clone | custom fusion | bytes 278528 | tf_op jit(solution)/shard_map/jit(_take)/gather | solution.py:37
  734.8 15.4 %gather_fusion.40 = f32[4096,8]{1,0:T(8,128)} fusion(f32[8,6144]{0,1:T(8,128)S(1)} %copy.178, s32[4096]{0:T(1024)} %fusion.89), kind=kCustom, calls=%fused_computation.41.clone | custom fusion | bytes 278528 | tf_op jit(solution)/shard_map/jit(_take)/gather | solution.py:37
  750.2 15.4 %gather_fusion.39 = f32[4096,8]{1,0:T(8,128)} fusion(f32[8,6144]{0,1:T(8,128)S(1)} %copy.178, s32[4096]{0:T(1024)} %fusion.88), kind=kCustom, calls=%fused_computation.40.clone | custom fusion | bytes 278528 | tf_op jit(solution)/shard_map/jit(_take)/gather | solution.py:37
  765.7 15.4 %gather_fusion.38 = f32[4096,8]{1,0:T(8,128)} fusion(f32[8,6144]{0,1:T(8,128)S(1)} %copy.178, s32[4096]{0:T(1024)} %fusion.87), kind=kCustom, calls=%fused_computation.39.clone | custom fusion | bytes 278528 | tf_op jit(solution)/shard_map/jit(_take)/gather | solution.py:37
  781.1 15.4 %gather_fusion.37 = f32[4096,8]{1,0:T(8,128)} fusion(f32[8,6144]{0,1:T(8,128)S(1)} %copy.178, s32[4096]{0:T(1024)} %fusion.86), kind=kCustom, calls=%fused_computation.38.clone | custom fusion | bytes 278528 | tf_op jit(solution)/shard_map/jit(_take)/gather | solution.py:37
  796.5 15.4 %gather_fusion.36 = f32[4096,8]{1,0:T(8,128)} fusion(f32[8,6144]{0,1:T(8,128)S(1)} %copy.178, s32[4096]{0:T(1024)} %fusion.85), kind=kCustom, calls=%fused_computation.37.clone | custom fusion | bytes 278528 | tf_op jit(solution)/shard_map/jit(_take)/gather | solution.py:37
  833.8 10.4 all_to_all.39
  846.7 15.4 %gather_fusion.48 = f32[4096,8]{1,0:T(8,128)} fusion(f32[8,6144]{0,1:T(8,128)S(1)} %copy.192, s32[4096]{0:T(1024)} %fusion.90), kind=kCustom, calls=%fused_computation.48.clone | custom fusion | bytes 278528 | tf_op jit(solution)/shard_map/jit(_take)/gather | solution.py:37
  862.2 15.4 %gather_fusion.47 = f32[4096,8]{1,0:T(8,128)} fusion(f32[8,6144]{0,1:T(8,128)S(1)} %copy.192, s32[4096]{0:T(1024)} %fusion.89), kind=kCustom, calls=%fused_computation.47.clone | custom fusion | bytes 278528 | tf_op jit(solution)/shard_map/jit(_take)/gather | solution.py:37
  877.6 15.4 %gather_fusion.46 = f32[4096,8]{1,0:T(8,128)} fusion(f32[8,6144]{0,1:T(8,128)S(1)} %copy.192, s32[4096]{0:T(1024)} %fusion.88), kind=kCustom, calls=%fused_computation.46.clone | custom fusion | bytes 278528 | tf_op jit(solution)/shard_map/jit(_take)/gather | solution.py:37
  893.0 15.4 %gather_fusion.45 = f32[4096,8]{1,0:T(8,128)} fusion(f32[8,6144]{0,1:T(8,128)S(1)} %copy.192, s32[4096]{0:T(1024)} %fusion.87), kind=kCustom, calls=%fused_computation.45.clone | custom fusion | bytes 278528 | tf_op jit(solution)/shard_map/jit(_take)/gather | solution.py:37
  908.4 15.4 %gather_fusion.44 = f32[4096,8]{1,0:T(8,128)} fusion(f32[8,6144]{0,1:T(8,128)S(1)} %copy.192, s32[4096]{0:T(1024)} %fusion.86), kind=kCustom, calls=%fused_computation.44.clone | custom fusion | bytes 278528 | tf_op jit(solution)/shard_map/jit(_take)/gather | solution.py:37
  923.8 15.4 %gather_fusion.43 = f32[4096,8]{1,0:T(8,128)} fusion(f32[8,6144]{0,1:T(8,128)S(1)} %copy.192, s32[4096]{0:T(1024)} %fusion.85), kind=kCustom, calls=%fused_computation.43.clone | custom fusion | bytes 278528 | tf_op jit(solution)/shard_map/jit(_take)/gather | solution.py:37
  954.5 92.4 %all-reduce.3.cloned.1.call-done = f32[128,4096]{1,0:T(8,128)} async-done(((f32[128,4096]{1,0:T(8,128)}), f32[128,4096]{1,0:T(8,128)}) %all-reduce.3.cloned.1.call-update) | async-done | bytes 2097168
  (398 shorter events, 230.6 us)
Async XLA Ops:
  6.5 943.2 %copy-start = (f32[128,128]{1,0:T(8,128)S(1)}, f32[128,128]{1,0:T(8,128)}, u32[]{:S(2)}) copy-start(f32[128,128]{1,0:T(8,128)} %param.13) | copy-start | bytes 196612
  6.5 56.2 %all-gather.2.cloned.1.call-start = ((), (), s32[]{:S(2)}) async-start(), calls=%async_computation.7 | async-start | bytes 2228224 | tf_op jit(solution)/shard_map/all_gather | solution.py:25
  11.1 54.3 %copy-start.115 = (f32[8]{0:T(128)}, f32[8]{0:T(128)S(1)}, u32[]{:S(2)}) copy-start(f32[8]{0:T(128)S(1)} %get-tuple-element.40) | copy-start | bytes 100
  65.4 130.4 %copy-start.19 = (f32[8,4096]{1,0:T(8,128)}, f32[8,4096]{1,0:T(8,128)S(1)}, u32[]{:S(2)}) copy-start(f32[8,4096]{1,0:T(8,128)S(1)} %get-tuple-element.42) | copy-start | bytes 393220
  72.5 10.5 copy-start.134
  72.5 10.5 copy-start.135
  72.5 10.5 copy-start.136
  74.5 16.3 %all-to-all-start = ((f32[8,16,128]{2,0,1:T(8,128)}), f32[8,16,128]{2,0,1:T(8,128)S(1)}, u32[]{:S(2)}, u32[]{:S(2)}) async-start(f32[8,16,128]{2,0,1:T(8,128)} %copy.107), calls=%async_computation | async-start | bytes 131072 | tf_op jit(solution)/shard_map/all_to_all | solution.py:31
  93.4 18.3 %copy-start.49 = (s32[4096]{0:T(1024)S(1)}, s32[4096]{0:T(1024)}, u32[]{:S(2)}) copy-start(s32[4096]{0:T(1024)} %fusion.89) | copy-start | bytes 49156
  111.6 16.9 %copy-start.47 = (s32[4096]{0:T(1024)S(1)}, s32[4096]{0:T(1024)}, u32[]{:S(2)}) copy-start(s32[4096]{0:T(1024)} %fusion.88) | copy-start | bytes 49156
  128.5 16.9 %copy-start.45 = (s32[4096]{0:T(1024)S(1)}, s32[4096]{0:T(1024)}, u32[]{:S(2)}) copy-start(s32[4096]{0:T(1024)} %fusion.87) | copy-start | bytes 49156
  145.4 16.9 %copy-start.41 = (s32[4096]{0:T(1024)S(1)}, s32[4096]{0:T(1024)}, u32[]{:S(2)}) copy-start(s32[4096]{0:T(1024)} %fusion.86) | copy-start | bytes 49156
  162.4 16.9 %copy-start.43 = (s32[4096]{0:T(1024)S(1)}, s32[4096]{0:T(1024)}, u32[]{:S(2)}) copy-start(s32[4096]{0:T(1024)} %fusion.85) | copy-start | bytes 49156
  205.3 13.1 %copy-start.51 = (s32[4096]{0:T(1024)S(1)}, s32[4096]{0:T(1024)}, u32[]{:S(2)}) copy-start(s32[4096]{0:T(1024)} %fusion.90) | copy-start | bytes 49156
  216.5 16.0 %copy-start.50 = (s32[4096]{0:T(1024)S(1)}, s32[4096]{0:T(1024)}, u32[]{:S(2)}) copy-start(s32[4096]{0:T(1024)} %fusion.89) | copy-start | bytes 49156
  216.5 30.1 %copy-start.48 = (s32[4096]{0:T(1024)S(1)}, s32[4096]{0:T(1024)}, u32[]{:S(2)}) copy-start(s32[4096]{0:T(1024)} %fusion.88) | copy-start | bytes 49156
  218.4 42.4 %copy-start.46 = (s32[4096]{0:T(1024)S(1)}, s32[4096]{0:T(1024)}, u32[]{:S(2)}) copy-start(s32[4096]{0:T(1024)} %fusion.87) | copy-start | bytes 49156
  218.4 56.4 %copy-start.42 = (s32[4096]{0:T(1024)S(1)}, s32[4096]{0:T(1024)}, u32[]{:S(2)}) copy-start(s32[4096]{0:T(1024)} %fusion.86) | copy-start | bytes 49156
  232.5 56.4 %copy-start.44 = (s32[4096]{0:T(1024)S(1)}, s32[4096]{0:T(1024)}, u32[]{:S(2)}) copy-start(s32[4096]{0:T(1024)} %fusion.85) | copy-start | bytes 49156
  321.3 5.6 copy-start.137
  323.2 11.4 %all-to-all-start.2 = ((f32[8,16,128]{2,0,1:T(8,128)}), f32[8,16,128]{2,0,1:T(8,128)S(1)}, u32[]{:S(2)}, u32[]{:S(2)}) async-start(f32[8,16,128]{2,0,1:T(8,128)} %copy.135), calls=%async_computation.2 | async-start | bytes 131072 | tf_op jit(solution)/shard_map/all_to_all | solution.py:31
  326.8 720.1 %all-reduce.3.cloned.1.call-start = ((), (), s32[]{:S(2)}) async-start(), calls=%async_computation.8 | async-start | bytes 4194304
  440.7 10.0 copy-start.106
  442.5 20.4 %copy-start.1 = (f32[8,4096]{1,0:T(8,128)}, f32[8,4096]{1,0:T(8,128)S(1)}, u32[]{:S(2)}) copy-start(f32[8,4096]{1,0:T(8,128)S(1)} %get-tuple-element.13) | copy-start | bytes 393220
  578.5 11.7 %copy-start.26 = (f32[8,4096]{1,0:T(8,128)S(1)}, f32[8,4096]{1,0:T(8,128)}, u32[]{:S(2)}) copy-start(f32[8,4096]{1,0:T(8,128)} %copy-done.25) | copy-start | bytes 393220
  695.5 9.2 copy-start.107
  696.5 20.4 %copy-start.4 = (f32[8,4096]{1,0:T(8,128)}, f32[8,4096]{1,0:T(8,128)S(1)}, u32[]{:S(2)}) copy-start(f32[8,4096]{1,0:T(8,128)S(1)} %get-tuple-element.9) | copy-start | bytes 393220
  817.0 4.7 copy-start.13
  832.4 11.8 %copy-start.24 = (f32[8,4096]{1,0:T(8,128)S(1)}, f32[8,4096]{1,0:T(8,128)}, u32[]{:S(2)}) copy-start(f32[8,4096]{1,0:T(8,128)} %copy-done.23) | copy-start | bytes 393220
  945.0 4.7 copy-start.3
  945.0 4.7 copy-start.6
  945.0 4.7 copy-start.20
  945.0 4.7 copy-start.22
  945.0 4.7 copy-start.33
  945.0 4.7 copy-start.40
  945.1 4.7 copy-start.54
  945.1 4.7 copy-start.70
  945.1 4.7 copy-start.77
  945.1 4.7 copy-start.84
  945.1 4.7 copy-start.91
  945.1 4.7 copy-start.98
  945.1 4.7 copy-start.105
  945.1 4.7 copy-start.114
  945.1 4.7 copy-start.119
  945.1 4.7 copy-start.122
  945.2 4.7 copy-start.125
  945.2 4.7 copy-start.131
  945.2 4.7 copy-start.133
  (95 other events, 302.1 us)
Sparse Core Ops, SparseCore 0:
  9.8 52.8 all-gather.1
  953.3 93.5 all-reduce.2
where the time goes:
time: 1070 us; the launch traced here: 1060 us
  local copies, waits for them, and re-layouts  788 us (74%)
  waiting for transfers between devices  149 us (14%)
  blocking collectives  52 us (5%)
  other arithmetic  32.2 us (3%)
  between operations  15.8 us (1%)
  starting transfers between devices  12.2 us (1%)
    gather x84, local copies, waits for them, and re-layouts, apply_operator(): jnp.take(extended, neighbours[slot_number], axis=1)  712 us
    unnamed x3, waiting for transfers between devices  93.1 us
    all_to_all x5, blocking collectives, apply_operator(): lax.all_to_all(outgoing.reshape(slab_rows, -1, HMAX), 'cells', split_axis...  52 us
    gather x7, local copies, waits for them, and re-layouts, apply_operator(): outgoing = jnp.take(field, send_cells, axis=1)  47.4 us
    all_gather x1, waiting for transfers between devices, local(): lax.all_gather(source_levels, 'lev', axis=0, tiled=True)  41.8 us
  transfers between devices with their start and end apart: 4, of which 4 were waited for; matrix products, arithmetic and copies ran while one was open for 1% of the time, Pallas kernels for 0%

commit v1 on v0

--- a/solution.py
+++ b/solution.py
@@ -22,7 +22,12 @@
     slot_total = send_cells.shape[0]
     diagonal = jnp.sum(edge_weight, axis=0)
     own_rows = lax.dynamic_slice_in_dim(level_to_mode, position * slab_rows, slab_rows, 0)
-    mode_field = full_product(own_rows, lax.all_gather(source_levels, "lev", axis=0, tiled=True))
+    mode_field = full_product(
+        own_rows,
+        jnp.concatenate(
+            lax.all_to_all(jnp.stack([source_levels] * lax.axis_size("lev")), "lev", 0, 0), axis=0
+        ),
+    )
     shift_col = mode_shift[:, None]
     own_scale = shift_col + diagonal[None, :]
 

time: 1070 us -> 1020 us (0.953)
  local copies, waits for them, and re-layouts: 788 us -> 759 us
  waiting for transfers between devices: 149 us -> 128 us
  starting transfers between devices: 12.2 us -> 23.1 us
    all_gather x1 -> x0, waiting for transfers between devices: 41.8 us -> none  [local(): lax.all_gather(source_levels, 'lev', axis=0, tiled=True)]
    gather x84, local copies, waits for them, and re-layouts: 712 us -> 684 us  [apply_operator(): jnp.take(extended, neighbours[slot_number], axis=1)]
    all_to_all x0 -> x1, waiting for transfers between devices: none -> 22.2 us  [local(): lax.all_to_all(jnp.stack([source_levels] * lax.axis_size('lev')), 'lev',...]
    unnamed x3 -> x2, waiting for transfers between devices: 93.1 us -> 91.2 us
where the time goes in v1:
time: 1020 us; the launch traced here: 1010 us
  local copies, waits for them, and re-layouts  759 us (74%)
  waiting for transfers between devices  128 us (13%)
  blocking collectives  52 us (5%)
  other arithmetic  27.3 us (3%)
  starting transfers between devices  23.1 us (2%)
  between operations  16.2 us (2%)
    gather x84, local copies, waits for them, and re-layouts, apply_operator(): jnp.take(extended, neighbours[slot_number], axis=1)  684 us
    unnamed x2, waiting for transfers between devices  91.2 us
    all_to_all x5, blocking collectives, apply_operator(): lax.all_to_all(outgoing.reshape(slab_rows, -1, HMAX), 'cells', split_axis...  52 us
    gather x7, local copies, waits for them, and re-layouts, apply_operator(): outgoing = jnp.take(field, send_cells, axis=1)  47.3 us
    all_to_all x1, waiting for transfers between devices, local(): lax.all_to_all(jnp.stack([source_levels] * lax.axis_size('lev')), 'lev',...  22.2 us
  transfers between devices with their start and end apart: 4, of which 4 were waited for; matrix products, arithmetic and copies ran while one was open for 1% of the time, Pallas kernels for 0%

profile of v1, /device:TPU:1, one launch (start us, length us, event | category | flops | bytes accessed | tf_op | source)
XLA Modules:
  0.0 1010.5 jit_solution(3349470779411193542)
XLA Ops:
  22.4 22.2 %all-to-all-done = f32[16,8,4096]{2,1,0:T(8,128)S(1)} async-done(((f32[16,8,4096]{2,1,0:T(8,128)}), f32[16,8,4096]{2,1,0:T(8,128)S(1)}, u32[]{:S(2)}, u32[]{:S(2)}) %all-to-all-start) | async-done | bytes 2097184 | tf_op jit(solution)/shard_map/all_to_all | solution.py:28
  55.4 11.9 %all-to-all-start.1 = ((f32[8,16,128]{2,0,1:T(8,128)}), f32[8,16,128]{2,0,1:T(8,128)S(1)}, u32[]{:S(2)}, u32[]{:S(2)}) async-start(f32[8,16,128]{2,0,1:T(8,128)} %copy.107), calls=%async_computation.1 | async-start | bytes 131072 | tf_op jit(solution)/shard_map/all_to_all | solution.py:36
  77.7 15.4 %gather_fusion.6 = f32[4096,8]{1,0:T(8,128)} fusion(f32[8,6144]{0,1:T(8,128)S(1)} %copy.108, s32[4096]{0:T(1024)} %fusion.92), kind=kCustom, calls=%fused_computation.12.clone | custom fusion | bytes 278528 | tf_op jit(solution)/shard_map/jit(_take)/gather | solution.py:42
  95.9 14.1 %gather_fusion.5 = f32[4096,8]{1,0:T(8,128)} fusion(f32[8,6144]{0,1:T(8,128)S(1)} %copy.108, s32[4096]{0:T(1024)S(1)} %fusion.91), kind=kCustom, calls=%fused_computation.11.clone | custom fusion | bytes 278528 | tf_op jit(solution)/shard_map/jit(_take)/gather | solution.py:42
  112.8 14.1 %gather_fusion.4 = f32[4096,8]{1,0:T(8,128)} fusion(f32[8,6144]{0,1:T(8,128)S(1)} %copy.108, s32[4096]{0:T(1024)S(1)} %fusion.90), kind=kCustom, calls=%fused_computation.10.clone | custom fusion | bytes 278528 | tf_op jit(solution)/shard_map/jit(_take)/gather | solution.py:42
  129.7 14.1 %gather_fusion.3 = f32[4096,8]{1,0:T(8,128)} fusion(f32[8,6144]{0,1:T(8,128)S(1)} %copy.108, s32[4096]{0:T(1024)S(1)} %fusion.89), kind=kCustom, calls=%fused_computation.9.clone | custom fusion | bytes 278528 | tf_op jit(solution)/shard_map/jit(_take)/gather | solution.py:42
  146.6 14.1 %gather_fusion.2 = f32[4096,8]{1,0:T(8,128)} fusion(f32[8,6144]{0,1:T(8,128)S(1)} %copy.108, s32[4096]{0:T(1024)S(1)} %fusion.88), kind=kCustom, calls=%fused_computation.8.clone | custom fusion | bytes 278528 | tf_op jit(solution)/shard_map/jit(_take)/gather | solution.py:42
  163.5 14.1 %gather_fusion.1 = f32[4096,8]{1,0:T(8,128)} fusion(f32[8,6144]{0,1:T(8,128)S(1)} %copy.108, s32[4096]{0:T(1024)S(1)} %copy-done.70), kind=kCustom, calls=%fused_computation.1.clone | custom fusion | bytes 278528 | tf_op jit(solution)/shard_map/jit(_take)/gather | solution.py:42
  189.6 10.5 %all_to_all.40 = f32[8,16,128]{2,0,1:T(8,128)S(1)} all-to-all(f32[8,16,128]{2,0,1:T(8,128)S(1)} %copy.121), channel_id=1, replica_groups=mesh['cells'=16,'lev'=16] {'cells'}, dimensions={1} | all-to-all | bytes 131072 | tf_op jit(solution)/shard_map/all_to_all | solution.py:36
  202.7 14.1 %gather_fusion.13 = f32[4096,8]{1,0:T(8,128)} fusion(f32[8,6144]{0,1:T(8,128)S(1)} %copy.122, s32[4096]{0:T(1024)S(1)} %copy-done.27), kind=kCustom, calls=%fused_computation.18.clone | custom fusion | bytes 278528 | tf_op jit(solution)/shard_map/jit(_take)/gather | solution.py:42
  216.8 14.1 %gather_fusion.12 = f32[4096,8]{1,0:T(8,128)} fusion(f32[8,6144]{0,1:T(8,128)S(1)} %copy.122, s32[4096]{0:T(1024)S(1)} %fusion.91), kind=kCustom, calls=%fused_computation.17.clone | custom fusion | bytes 278528 | tf_op jit(solution)/shard_map/jit(_take)/gather | solution.py:42
  230.8 14.1 %gather_fusion.11 = f32[4096,8]{1,0:T(8,128)} fusion(f32[8,6144]{0,1:T(8,128)S(1)} %copy.122, s32[4096]{0:T(1024)S(1)} %fusion.90), kind=kCustom, calls=%fused_computation.16.clone | custom fusion | bytes 278528 | tf_op jit(solution)/shard_map/jit(_take)/gather | solution.py:42
  244.9 14.1 %gather_fusion.10 = f32[4096,8]{1,0:T(8,128)} fusion(f32[8,6144]{0,1:T(8,128)S(1)} %copy.122, s32[4096]{0:T(1024)S(1)} %fusion.89), kind=kCustom, calls=%fused_computation.15.clone | custom fusion | bytes 278528 | tf_op jit(solution)/shard_map/jit(_take)/gather | solution.py:42
  258.9 14.1 %gather_fusion.9 = f32[4096,8]{1,0:T(8,128)} fusion(f32[8,6144]{0,1:T(8,128)S(1)} %copy.122, s32[4096]{0:T(1024)S(1)} %fusion.88), kind=kCustom, calls=%fused_computation.14.clone | custom fusion | bytes 278528 | tf_op jit(solution)/shard_map/jit(_take)/gather | solution.py:42
  273.0 14.1 %gather_fusion.8 = f32[4096,8]{1,0:T(8,128)} fusion(f32[8,6144]{0,1:T(8,128)S(1)} %copy.122, s32[4096]{0:T(1024)S(1)} %copy-done.71), kind=kCustom, calls=%fused_computation.13.clone | custom fusion | bytes 278528 | tf_op jit(solution)/shard_map/jit(_take)/gather | solution.py:42
  321.2 15.4 %gather_fusion.20 = f32[4096,8]{1,0:T(8,128)} fusion(f32[8,6144]{0,1:T(8,128)S(1)} %copy.136, s32[4096]{0:T(1024)} %fusion.92), kind=kCustom, calls=%fused_computation.24.clone | custom fusion | bytes 278528 | tf_op jit(solution)/shard_map/jit(_take)/gather | solution.py:42
  336.6 14.1 %gather_fusion.19 = f32[4096,8]{1,0:T(8,128)} fusion(f32[8,6144]{0,1:T(8,128)S(1)} %copy.136, s32[4096]{0:T(1024)S(1)} %fusion.91), kind=kCustom, calls=%fused_computation.23.clone | custom fusion | bytes 278528 | tf_op jit(solution)/shard_map/jit(_take)/gather | solution.py:42
  350.6 14.1 %gather_fusion.18 = f32[4096,8]{1,0:T(8,128)} fusion(f32[8,6144]{0,1:T(8,128)S(1)} %copy.136, s32[4096]{0:T(1024)S(1)} %fusion.90), kind=kCustom, calls=%fused_computation.22.clone | custom fusion | bytes 278528 | tf_op jit(solution)/shard_map/jit(_take)/gather | solution.py:42
  364.7 14.1 %gather_fusion.17 = f32[4096,8]{1,0:T(8,128)} fusion(f32[8,6144]{0,1:T(8,128)S(1)} %copy.136, s32[4096]{0:T(1024)S(1)} %fusion.89), kind=kCustom, calls=%fused_computation.21.clone | custom fusion | bytes 278528 | tf_op jit(solution)/shard_map/jit(_take)/gather | solution.py:42
  378.8 14.1 %gather_fusion.16 = f32[4096,8]{1,0:T(8,128)} fusion(f32[8,6144]{0,1:T(8,128)S(1)} %copy.136, s32[4096]{0:T(1024)S(1)} %fusion.88), kind=kCustom, calls=%fused_computation.20.clone | custom fusion | bytes 278528 | tf_op jit(solution)/shard_map/jit(_take)/gather | solution.py:42
  392.8 15.4 %gather_fusion.15 = f32[4096,8]{1,0:T(8,128)} fusion(f32[8,6144]{0,1:T(8,128)S(1)} %copy.136, s32[4096]{0:T(1024)} %fusion.87), kind=kCustom, calls=%fused_computation.19.clone | custom fusion | bytes 278528 | tf_op jit(solution)/shard_map/jit(_take)/gather | solution.py:42
  431.2 10.4 %all_to_all.41 = f32[8,16,128]{2,0,1:T(8,128)S(1)} all-to-all(f32[8,16,128]{2,0,1:T(8,128)S(1)} %copy.149), channel_id=1, replica_groups=mesh['cells'=16,'lev'=16] {'cells'}, dimensions={1} | all-to-all | bytes 131072 | tf_op jit(solution)/shard_map/all_to_all | solution.py:36
  444.1 15.4 %gather_fusion.27 = f32[4096,8]{1,0:T(8,128)} fusion(f32[8,6144]{0,1:T(8,128)S(1)} %copy.150, s32[4096]{0:T(1024)} %fusion.92), kind=kCustom, calls=%fused_computation.30.clone | custom fusion | bytes 278528 | tf_op jit(solution)/shard_map/jit(_take)/gather | solution.py:42
  459.5 14.1 %gather_fusion.26 = f32[4096,8]{1,0:T(8,128)} fusion(f32[8,6144]{0,1:T(8,128)S(1)} %copy.150, s32[4096]{0:T(1024)S(1)} %fusion.91), kind=kCustom, calls=%fused_computation.29.clone | custom fusion | bytes 278528 | tf_op jit(solution)/shard_map/jit(_take)/gather | solution.py:42
  473.6 14.1 %gather_fusion.25 = f32[4096,8]{1,0:T(8,128)} fusion(f32[8,6144]{0,1:T(8,128)S(1)} %copy.150, s32[4096]{0:T(1024)S(1)} %fusion.90), kind=kCustom, calls=%fused_computation.28.clone | custom fusion | bytes 278528 | tf_op jit(solution)/shard_map/jit(_take)/gather | solution.py:42
  487.6 14.1 %gather_fusion.24 = f32[4096,8]{1,0:T(8,128)} fusion(f32[8,6144]{0,1:T(8,128)S(1)} %copy.150, s32[4096]{0:T(1024)S(1)} %fusion.89), kind=kCustom, calls=%fused_computation.27.clone | custom fusion | bytes 278528 | tf_op jit(solution)/shard_map/jit(_take)/gather | solution.py:42
  501.7 14.1 %gather_fusion.23 = f32[4096,8]{1,0:T(8,128)} fusion(f32[8,6144]{0,1:T(8,128)S(1)} %copy.150, s32[4096]{0:T(1024)S(1)} %fusion.88), kind=kCustom, calls=%fused_computation.26.clone | custom fusion | bytes 278528 | tf_op jit(solution)/shard_map/jit(_take)/gather | solution.py:42
  515.8 15.4 %gather_fusion.22 = f32[4096,8]{1,0:T(8,128)} fusion(f32[8,6144]{0,1:T(8,128)S(1)} %copy.150, s32[4096]{0:T(1024)} %fusion.87), kind=kCustom, calls=%fused_computation.25.clone | custom fusion | bytes 278528 | tf_op jit(solution)/shard_map/jit(_take)/gather | solution.py:42
  565.9 15.4 %gather_fusion.34 = f32[4096,8]{1,0:T(8,128)} fusion(f32[8,6144]{0,1:T(8,128)S(1)} %copy.164, s32[4096]{0:T(1024)} %fusion.92), kind=kCustom, calls=%fused_computation.36.clone | custom fusion | bytes 278528 | tf_op jit(solution)/shard_map/jit(_take)/gather | solution.py:42
  581.4 14.1 %gather_fusion.33 = f32[4096,8]{1,0:T(8,128)} fusion(f32[8,6144]{0,1:T(8,128)S(1)} %copy.164, s32[4096]{0:T(1024)S(1)} %fusion.91), kind=kCustom, calls=%fused_computation.35.clone | custom fusion | bytes 278528 | tf_op jit(solution)/shard_map/jit(_take)/gather | solution.py:42
  595.4 14.1 %gather_fusion.32 = f32[4096,8]{1,0:T(8,128)} fusion(f32[8,6144]{0,1:T(8,128)S(1)} %copy.164, s32[4096]{0:T(1024)S(1)} %fusion.90), kind=kCustom, calls=%fused_computation.34.clone | custom fusion | bytes 278528 | tf_op jit(solution)/shard_map/jit(_take)/gather | solution.py:42
  609.5 14.1 %gather_fusion.31 = f32[4096,8]{1,0:T(8,128)} fusion(f32[8,6144]{0,1:T(8,128)S(1)} %copy.164, s32[4096]{0:T(1024)S(1)} %fusion.89), kind=kCustom, calls=%fused_computation.33.clone | custom fusion | bytes 278528 | tf_op jit(solution)/shard_map/jit(_take)/gather | solution.py:42
  623.5 14.1 %gather_fusion.30 = f32[4096,8]{1,0:T(8,128)} fusion(f32[8,6144]{0,1:T(8,128)S(1)} %copy.164, s32[4096]{0:T(1024)S(1)} %fusion.88), kind=kCustom, calls=%fused_computation.32.clone | custom fusion | bytes 278528 | tf_op jit(solution)/shard_map/jit(_take)/gather | solution.py:42
  637.6 15.4 %gather_fusion.29 = f32[4096,8]{1,0:T(8,128)} fusion(f32[8,6144]{0,1:T(8,128)S(1)} %copy.164, s32[4096]{0:T(1024)} %fusion.87), kind=kCustom, calls=%fused_computation.31.clone | custom fusion | bytes 278528 | tf_op jit(solution)/shard_map/jit(_take)/gather | solution.py:42
  675.0 10.4 %all_to_all.43 = f32[8,16,128]{2,0,1:T(8,128)S(1)} all-to-all(f32[8,16,128]{2,0,1:T(8,128)S(1)} %copy.177), channel_id=1, replica_groups=mesh['cells'=16,'lev'=16] {'cells'}, dimensions={1} | all-to-all | bytes 131072 | tf_op jit(solution)/shard_map/all_to_all | solution.py:36
  688.0 15.4 %gather_fusion.41 = f32[4096,8]{1,0:T(8,128)} fusion(f32[8,6144]{0,1:T(8,128)S(1)} %copy.178, s32[4096]{0:T(1024)} %fusion.92), kind=kCustom, calls=%fused_computation.42.clone | custom fusion | bytes 278528 | tf_op jit(solution)/shard_map/jit(_take)/gather | solution.py:42
  703.4 14.1 %gather_fusion.40 = f32[4096,8]{1,0:T(8,128)} fusion(f32[8,6144]{0,1:T(8,128)S(1)} %copy.178, s32[4096]{0:T(1024)S(1)} %fusion.91), kind=kCustom, calls=%fused_computation.41.clone | custom fusion | bytes 278528 | tf_op jit(solution)/shard_map/jit(_take)/gather | solution.py:42
  717.4 14.1 %gather_fusion.39 = f32[4096,8]{1,0:T(8,128)} fusion(f32[8,6144]{0,1:T(8,128)S(1)} %copy.178, s32[4096]{0:T(1024)S(1)} %fusion.90), kind=kCustom, calls=%fused_computation.40.clone | custom fusion | bytes 278528 | tf_op jit(solution)/shard_map/jit(_take)/gather | solution.py:42
  731.5 14.1 %gather_fusion.38 = f32[4096,8]{1,0:T(8,128)} fusion(f32[8,6144]{0,1:T(8,128)S(1)} %copy.178, s32[4096]{0:T(1024)S(1)} %fusion.89), kind=kCustom, calls=%fused_computation.39.clone | custom fusion | bytes 278528 | tf_op jit(solution)/shard_map/jit(_take)/gather | solution.py:42
  745.6 14.1 %gather_fusion.37 = f32[4096,8]{1,0:T(8,128)} fusion(f32[8,6144]{0,1:T(8,128)S(1)} %copy.178, s32[4096]{0:T(1024)S(1)} %fusion.88), kind=kCustom, calls=%fused_computation.38.clone | custom fusion | bytes 278528 | tf_op jit(solution)/shard_map/jit(_take)/gather | solution.py:42
  759.6 15.4 %gather_fusion.36 = f32[4096,8]{1,0:T(8,128)} fusion(f32[8,6144]{0,1:T(8,128)S(1)} %copy.178, s32[4096]{0:T(1024)} %fusion.87), kind=kCustom, calls=%fused_computation.37.clone | custom fusion | bytes 278528 | tf_op jit(solution)/shard_map/jit(_take)/gather | solution.py:42
  809.8 15.4 %gather_fusion.48 = f32[4096,8]{1,0:T(8,128)} fusion(f32[8,6144]{0,1:T(8,128)S(1)} %copy.192, s32[4096]{0:T(1024)} %fusion.92), kind=kCustom, calls=%fused_computation.48.clone | custom fusion | bytes 278528 | tf_op jit(solution)/shard_map/jit(_take)/gather | solution.py:42
  825.3 14.1 %gather_fusion.47 = f32[4096,8]{1,0:T(8,128)} fusion(f32[8,6144]{0,1:T(8,128)S(1)} %copy.192, s32[4096]{0:T(1024)S(1)} %fusion.91), kind=kCustom, calls=%fused_computation.47.clone | custom fusion | bytes 278528 | tf_op jit(solution)/shard_map/jit(_take)/gather | solution.py:42
  839.3 14.1 %gather_fusion.46 = f32[4096,8]{1,0:T(8,128)} fusion(f32[8,6144]{0,1:T(8,128)S(1)} %copy.192, s32[4096]{0:T(1024)S(1)} %fusion.90), kind=kCustom, calls=%fused_computation.46.clone | custom fusion | bytes 278528 | tf_op jit(solution)/shard_map/jit(_take)/gather | solution.py:42
  853.4 14.1 %gather_fusion.45 = f32[4096,8]{1,0:T(8,128)} fusion(f32[8,6144]{0,1:T(8,128)S(1)} %copy.192, s32[4096]{0:T(1024)S(1)} %fusion.89), kind=kCustom, calls=%fused_computation.45.clone | custom fusion | bytes 278528 | tf_op jit(solution)/shard_map/jit(_take)/gather | solution.py:42
  867.4 14.1 %gather_fusion.44 = f32[4096,8]{1,0:T(8,128)} fusion(f32[8,6144]{0,1:T(8,128)S(1)} %copy.192, s32[4096]{0:T(1024)S(1)} %fusion.88), kind=kCustom, calls=%fused_computation.44.clone | custom fusion | bytes 278528 | tf_op jit(solution)/shard_map/jit(_take)/gather | solution.py:42
  881.5 14.1 %gather_fusion.43 = f32[4096,8]{1,0:T(8,128)} fusion(f32[8,6144]{0,1:T(8,128)S(1)} %copy.192, s32[4096]{0:T(1024)S(1)} %copy-done.72), kind=kCustom, calls=%fused_computation.43.clone | custom fusion | bytes 278528 | tf_op jit(solution)/shard_map/jit(_take)/gather | solution.py:42
  910.9 91.1 %all-reduce.3.cloned.1.call-done = f32[128,4096]{1,0:T(8,128)} async-done(((f32[128,4096]{1,0:T(8,128)}), f32[128,4096]{1,0:T(8,128)}) %all-reduce.3.cloned.1.call-update) | async-done | bytes 2097168
  (436 shorter events, 233.4 us)
Async XLA Ops:
  6.5 899.6 %copy-start = (f32[128,128]{1,0:T(8,128)S(1)}, f32[128,128]{1,0:T(8,128)}, u32[]{:S(2)}) copy-start(f32[128,128]{1,0:T(8,128)} %param.13) | copy-start | bytes 196612
  9.0 7.8 copy-start.137
  9.0 8.9 copy-start.129
  9.0 9.6 copy-start.85
  9.0 9.7 copy-start.130
  9.0 35.6 %all-to-all-start = ((f32[16,8,4096]{2,1,0:T(8,128)}), f32[16,8,4096]{2,1,0:T(8,128)S(1)}, u32[]{:S(2)}, u32[]{:S(2)}) async-start(f32[16,8,4096]{2,1,0:T(8,128)} %stack.2), calls=%async_computation | async-start | bytes 4194304 | tf_op jit(solution)/shard_map/all_to_all | solution.py:28
  19.3 27.1 %copy-start.138 = (f32[8]{0:T(128)}, f32[8]{0:T(128)S(1)}, u32[]{:S(2)}) copy-start(f32[8]{0:T(128)S(1)} %get-tuple-element.40) | copy-start | bytes 100
  46.4 133.8 %copy-start.19 = (f32[8,4096]{1,0:T(8,128)}, f32[8,4096]{1,0:T(8,128)S(1)}, u32[]{:S(2)}) copy-start(f32[8,4096]{1,0:T(8,128)S(1)} %get-tuple-element.42) | copy-start | bytes 393220
  53.5 13.9 %copy-start.153 = (f32[8]{0:T(128)S(1)}, f32[8]{0:T(128)}, u32[]{:S(2)}) copy-start(f32[8]{0:T(128)} %get-tuple-element.17) | copy-start | bytes 100
  53.5 13.9 %copy-start.154 = (f32[8]{0:T(128)S(1)}, f32[8]{0:T(128)}, u32[]{:S(2)}) copy-start(f32[8]{0:T(128)} %get-tuple-element.18) | copy-start | bytes 100
  53.5 13.9 %copy-start.155 = (f32[8]{0:T(128)S(1)}, f32[8]{0:T(128)}, u32[]{:S(2)}) copy-start(f32[8]{0:T(128)} %get-tuple-element.19) | copy-start | bytes 100
  55.4 19.7 %all-to-all-start.1 = ((f32[8,16,128]{2,0,1:T(8,128)}), f32[8,16,128]{2,0,1:T(8,128)S(1)}, u32[]{:S(2)}, u32[]{:S(2)}) async-start(f32[8,16,128]{2,0,1:T(8,128)} %copy.107), calls=%async_computation.1 | async-start | bytes 131072 | tf_op jit(solution)/shard_map/all_to_all | solution.py:36
  146.6 16.9 %copy-start.70 = (s32[4096]{0:T(1024)S(1)}, s32[4096]{0:T(1024)}, u32[]{:S(2)}) copy-start(s32[4096]{0:T(1024)} %fusion.87) | copy-start | bytes 49156
  189.6 13.1 %copy-start.27 = (s32[4096]{0:T(1024)S(1)}, s32[4096]{0:T(1024)}, u32[]{:S(2)}) copy-start(s32[4096]{0:T(1024)} %fusion.92) | copy-start | bytes 49156
  216.8 56.2 %copy-start.71 = (s32[4096]{0:T(1024)S(1)}, s32[4096]{0:T(1024)}, u32[]{:S(2)}) copy-start(s32[4096]{0:T(1024)} %fusion.87) | copy-start | bytes 49156
  305.5 5.4 copy-start.156
  307.3 11.3 %all-to-all-start.3 = ((f32[8,16,128]{2,0,1:T(8,128)}), f32[8,16,128]{2,0,1:T(8,128)S(1)}, u32[]{:S(2)}, u32[]{:S(2)}) async-start(f32[8,16,128]{2,0,1:T(8,128)} %copy.135), calls=%async_computation.3 | async-start | bytes 131072 | tf_op jit(solution)/shard_map/all_to_all | solution.py:36
  310.8 691.3 %all-reduce.3.cloned.1.call-start = ((), (), s32[]{:S(2)}) async-start(), calls=%async_computation.8 | async-start | bytes 4194304
  419.3 10.0 copy-start.128
  421.1 20.4 %copy-start.1 = (f32[8,4096]{1,0:T(8,128)}, f32[8,4096]{1,0:T(8,128)S(1)}, u32[]{:S(2)}) copy-start(f32[8,4096]{1,0:T(8,128)S(1)} %get-tuple-element.13) | copy-start | bytes 393220
  536.2 4.7 copy-start.11
  551.8 11.6 %copy-start.26 = (f32[8,4096]{1,0:T(8,128)S(1)}, f32[8,4096]{1,0:T(8,128)}, u32[]{:S(2)}) copy-start(f32[8,4096]{1,0:T(8,128)} %copy-done.25) | copy-start | bytes 393220
  665.0 20.4 %copy-start.4 = (f32[8,4096]{1,0:T(8,128)}, f32[8,4096]{1,0:T(8,128)S(1)}, u32[]{:S(2)}) copy-start(f32[8,4096]{1,0:T(8,128)S(1)} %get-tuple-element.9) | copy-start | bytes 393220
  795.6 11.7 %copy-start.24 = (f32[8,4096]{1,0:T(8,128)S(1)}, f32[8,4096]{1,0:T(8,128)}, u32[]{:S(2)}) copy-start(f32[8,4096]{1,0:T(8,128)} %copy-done.23) | copy-start | bytes 393220
  839.3 42.2 %copy-start.72 = (s32[4096]{0:T(1024)S(1)}, s32[4096]{0:T(1024)}, u32[]{:S(2)}) copy-start(s32[4096]{0:T(1024)} %fusion.87) | copy-start | bytes 49156
  901.4 4.7 copy-start.3
  901.4 4.8 copy-start.6
  901.4 4.8 copy-start.20
  901.4 4.8 copy-start.22
  901.4 4.8 copy-start.34
  901.4 4.8 copy-start.41
  901.4 4.8 copy-start.48
  901.4 4.8 copy-start.55
  901.4 4.8 copy-start.62
  901.4 4.8 copy-start.69
  901.4 4.8 copy-start.75
  901.5 4.8 copy-start.92
  901.5 4.8 copy-start.99
  901.5 4.8 copy-start.106
  901.5 4.8 copy-start.113
  901.5 4.8 copy-start.120
  901.5 4.8 copy-start.127
  901.5 4.8 copy-start.136
  901.5 4.8 copy-start.141
  901.5 4.8 copy-start.144
  901.6 4.8 copy-start.146
  901.6 4.8 copy-start.150
  901.6 4.8 copy-start.152
  (114 other events, 369.8 us)
Sparse Core Ops, SparseCore 0:
  909.8 92.2 all-reduce.2
